TPU v7x, 512 devices: a whole 4x4x16 slice. The times are simulated.
512 devices in a mesh: leaf: 128 (over z, x, core), vec: 4 (over y).
Axes of the slice: x: 4, y: 4, z: 16, core: 2. Of those that a mesh axis runs over, the one named last changes fastest.
Arguments:
- samples: bfloat16 [64, 524288], P('vec', 'leaf'), may hold values from -6 to 6
- coords: float32 [3, 524288], P(None, 'leaf'), may hold values from -4 to 4
- panel_area: float32 [524288], P('leaf'), may hold values from 0.05 to 0.5
- quad_weight: float32 [524288], P('leaf'), may hold values from 0.2 to 1
- leaf_basis: bfloat16 [2048, 64, 256], P('leaf'), may hold values from -0.375 to 0.375
- transfer: bfloat16 [1024, 2, 64, 64], P('leaf'), may hold values from -0.5 to 0.5
- coupling_fine: bfloat16 [2048, 16, 64, 64], P('leaf'), may hold values from -0.1875 to 0.1875
- coupling_coarse: bfloat16 [1024, 16, 64, 64], P('leaf'), may hold values from -0.1875 to 0.1875
- near_list: int32 [2048, 16], P('leaf'), may hold values from 0 to 2047, as said below
- send_fine: int32 [16384, 2], P('leaf'), may hold values from 0 to 15
- send_coarse: int32 [16384, 1], P('leaf'), may hold values from 0 to 7
- far_fine: int32 [2048, 16], P('leaf'), may hold values from 0 to 255, as said below
- far_coarse: int32 [1024, 16], P('leaf'), may hold values from 0 to 127, as said below
Outputs:
- sample_out: bfloat16 [64, 524288], P('vec', 'leaf')
- sample_gram: float32 [2048, 64, 64], P('leaf', 'vec')
Inputs may be any that keep to these rules, and one draw needn't show every extreme that they name: `near_list`: row g names 16 different leaves, each at most 16 leaves from g. `send_fine`: row e * 128 + d names clusters of device e, counted on e from 0; every slot carries one. `send_coarse`: row e * 128 + d names clusters of device e, counted on e from 0; every slot carries one. `far_fine`: the rows of one device's 16 leaves name each of the values 0 to 255 exactly once. `far_coarse`: the rows of one device's parents name each of the values 0 to 127 exactly once.
All inputs are finite; a program needn't handle non-finite values.
Results may differ from a plain program's by a relative error of at most 0.0085.
Values may be sent and summed in bfloat16 or wider, within the bound.
No kernel may reach another device: no remote copies, remote signals or barrier semaphores. Data moves between devices by JAX's collectives and lax.ppermute only.
A program may use at most 64 MiB of HBM per device.

v0:
```python
import jax
import jax.numpy as jnp
from jax import lax
from jax.sharding import PartitionSpec as P

LEAF = 256
HW = 16
four_pi = 4.0 * 3.141592653589793


def extended(block, sides, width):
    for axis, dim in sides:
        count = lax.axis_size(axis)
        forward = [(i, i + 1) for i in range(count - 1)]
        backward = [(target, source) for source, target in forward]
        low = lax.ppermute(
            lax.slice_in_dim(block, block.shape[dim] - width, None, axis=dim), axis, forward
        )
        high = lax.ppermute(lax.slice_in_dim(block, 0, width, axis=dim), axis, backward)
        block = jnp.concatenate([low, block, high], axis=dim)
    return block


def laid_out(blocks, dim):
    dims = list(blocks.shape[1:])
    dims[dim] *= blocks.shape[0]
    return jnp.moveaxis(blocks, 0, dim).reshape(dims)


def copy_for_each(array, axis):
    copies = jnp.broadcast_to(array, (lax.axis_size(axis), *array.shape))
    return lax.all_to_all(copies, axis, split_axis=0, concat_axis=0, tiled=True)


def gathered_copies(array, axis, dim):
    return laid_out(copy_for_each(array, axis), dim)


def kernel_block(target, source):
    delta_x = target[0][:, None] - source[0][None, :]
    delta_y = target[1][:, None] - source[1][None, :]
    delta_z = target[2][:, None] - source[2][None, :]
    distance = delta_x * delta_x + delta_y * delta_y + delta_z * delta_z + source[3][None, :]
    return (source[4][None, :] / (four_pi * jnp.sqrt(distance))).astype(jnp.bfloat16)


def apply_coupling(tile_set, received, far_list, vec_dev, basis_rank):
    coef_table = received.reshape(-1, vec_dev, basis_rank)
    picked = coef_table[far_list]
    return jnp.einsum("ibkl,ibvl->ivk", tile_set, picked, preferred_element_type=jnp.float32)


def near_leaves(leaf_ids, window, geo_leaves, vec_leaves, targets):

    def one_leaf(index):
        chosen = window[index]
        src_geo = jnp.take(geo_leaves, chosen, axis=1)
        src_vec = jnp.take(vec_leaves, chosen, axis=1)
        target = lax.dynamic_index_in_dim(targets, index, 1, keepdims=False)
        blocks = jax.vmap(kernel_block, (None, 1))(target, src_geo)
        return jnp.einsum("npq,vnq->vp", blocks, src_vec, preferred_element_type=jnp.float32)

    return lax.map(one_leaf, leaf_ids)


def per_device(
    samples,
    coords,
    panel_area,
    quad_weight,
    leaf_basis,
    transfer,
    coupling_fine,
    coupling_coarse,
    near_list,
    send_fine,
    send_coarse,
    far_fine,
    far_coarse,
):
    vec_dev, points = samples.shape
    leaf_dev, basis_rank, leaf_pts = leaf_basis.shape
    devices = lax.axis_size("leaf")
    device = lax.axis_index("leaf")
    geometry = jnp.concatenate([coords, panel_area[None, :], quad_weight[None, :]], axis=0)
    geo_wide = extended(geometry, (("leaf", 1),), HW * leaf_pts)
    vec_wide = extended(samples, (("leaf", 1),), HW * leaf_pts)
    geo_leaves = geo_wide.reshape(5, -1, leaf_pts)
    window = near_list - (device * leaf_dev - HW)
    targets = coords.reshape(3, leaf_dev, leaf_pts)
    local_rows = samples.reshape(vec_dev, leaf_dev, leaf_pts)
    fine_coef = jnp.einsum(
        "ikp,vip->ivk", leaf_basis, local_rows, preferred_element_type=jnp.float32
    ).astype(jnp.bfloat16)
    coarse_coef = jnp.einsum(
        "mskl,msvk->mvl",
        transfer,
        fine_coef.reshape(-1, 2, vec_dev, basis_rank),
        preferred_element_type=jnp.float32,
    ).astype(jnp.bfloat16)
    send_leafs = fine_coef[send_fine].reshape(devices, -1, vec_dev * basis_rank)
    send_parents = coarse_coef[send_coarse].reshape(devices, -1, vec_dev * basis_rank)
    got_leafs = lax.all_to_all(send_leafs, "leaf", split_axis=0, concat_axis=0, tiled=True)
    got_parents = lax.all_to_all(send_parents, "leaf", split_axis=0, concat_axis=0, tiled=True)
    vec_groups = lax.axis_size("vec")
    quarter = leaf_dev // vec_groups
    all_wide = gathered_copies(vec_wide, "vec", 0)
    all_leaves = all_wide.reshape(all_wide.shape[0], -1, leaf_pts)
    first_leaf = lax.axis_index("vec") * quarter
    leaf_ids = first_leaf + jnp.arange(quarter, dtype=jnp.int32)
    near_quarter = near_leaves(leaf_ids, window, geo_leaves, all_leaves, targets)
    near_part = lax.all_to_all(
        near_quarter.astype(jnp.bfloat16), "vec", split_axis=1, concat_axis=0, tiled=True
    ).astype(near_quarter.dtype)
    field_fine = apply_coupling(coupling_fine, got_leafs, far_fine, vec_dev, basis_rank)
    field_coarse = apply_coupling(
        coupling_coarse, got_parents, far_coarse, vec_dev, basis_rank
    ).astype(jnp.bfloat16)
    pushed = jnp.einsum(
        "mskl,mvl->msvk", transfer, field_coarse, preferred_element_type=jnp.float32
    )
    local_field = (field_fine + pushed.reshape(leaf_dev, vec_dev, basis_rank)).astype(jnp.bfloat16)
    far_part = jnp.einsum(
        "ikp,ivk->vip", leaf_basis, local_field, preferred_element_type=jnp.float32
    )
    sample_out = (
        (jnp.transpose(near_part, (1, 0, 2)) + far_part)
        .reshape(vec_dev, points)
        .astype(jnp.bfloat16)
    )
    own_rows = sample_out.reshape(vec_dev, leaf_dev, leaf_pts)
    shard_rows = gathered_copies(sample_out, "vec", 0)
    shaped = shard_rows.reshape(shard_rows.shape[0], leaf_dev, leaf_pts)
    sample_gram = jnp.einsum(
        "vip,wip->ivw", own_rows, shaped, preferred_element_type=jnp.float32
    ) * (1.0 / LEAF)
    return (sample_out, sample_gram)


def solution(mesh):
    return jax.shard_map(
        per_device,
        mesh=mesh,
        in_specs=(
            P("vec", "leaf"),
            P(None, "leaf"),
            P("leaf"),
            P("leaf"),
            P("leaf", None, None),
            P("leaf", None, None, None),
            P("leaf", None, None, None),
            P("leaf", None, None, None),
            P("leaf", None),
            P("leaf", None),
            P("leaf", None),
            P("leaf", None),
            P("leaf", None),
        ),
        out_specs=(P("vec", "leaf"), P("leaf", "vec", None)),
        check_vma=False,
    )
```

profile of v0, /device:TPU:32, one launch (start us, length us, event | category | flops | bytes accessed | tf_op | source)
XLA Modules:
  0.0 212.3 jit_solution(4894522826093835305)
XLA Ops:
  0.7 3.8 %collective-permute-start.1 = (bf16[16,4096]{1,0:T(8,128)(2,1)}, bf16[16,4096]{1,0:T(8,128)(2,1)}, u32[]{:S(2)}, u32[]{:S(2)}) collective-permute-start(bf16[16,4096]{1,0:T(8,128)(2,1)} %param.15), channel_id=1, source_target_pairs={{4,0},{8,4},{12,8},{16,12},{20,16},{24,20},{28,24},{32,28},{36,32}... | collective-permute-start | bytes 393224 | tf_op jit(solution)/shard_map/ppermute | solution.py:19
  4.5 1.9 collective-permute-start
  6.4 0.9 pad_maximum_fusion.2
  7.3 5.8 %collective-permute-start.3 = (f32[5,4096]{1,0:T(8,128)S(1)}, f32[5,4096]{1,0:T(8,128)S(1)}, u32[]{:S(2)}, u32[]{:S(2)}) collective-permute-start(f32[5,4096]{1,0:T(8,128)S(1)} %pad_maximum_fusion.2), channel_id=1, source_target_pairs={{4,0},{8,4},{12,8},{16,12},{20,16},{24,20},{28,24},{32,28},{36,32}... | collective-permute-start | bytes 245768 | tf_op jit(solution)/shard_map/ppermute | solution.py:19
  13.1 1.9 collective-permute-start.2
  16.3 1.3 broadcast_subtract_fusion
  17.6 1.3 convolution_convert_fusion
  19.0 1.2 fusion.12
  20.2 1.5 copy.72
  24.3 0.9 reshape.159
  26.5 1.0 pad_maximum_fusion
  27.5 1.2 broadcast_in_dim.52
  28.8 4.5 %all-to-all-start = ((bf16[4,16,12288]{2,1,0:T(8,128)(2,1)}), bf16[4,16,12288]{2,1,0:T(8,128)(2,1)}, u32[]{:S(2)}, u32[]{:S(2)}) async-start(bf16[4,16,12288]{2,1,0:T(8,128)(2,1)} %broadcast_in_dim.52), calls=%async_computation | async-start | bytes 3145728 | tf_op jit(solution)/shard_map/all_to_all | solution.py:32
  33.3 1.0 pad_maximum_fusion.1
  34.3 17.8 %all-to-all-done = bf16[4,16,12288]{2,1,0:T(8,128)(2,1)} async-done(((bf16[4,16,12288]{2,1,0:T(8,128)(2,1)}), bf16[4,16,12288]{2,1,0:T(8,128)(2,1)}, u32[]{:S(2)}, u32[]{:S(2)}) %all-to-all-start) | async-done | bytes 1572896 | tf_op jit(solution)/shard_map/all_to_all | solution.py:32
  52.1 19.6 %all-to-all-start.3 = ((bf16[128,2,512]{2,1,0:T(2,128)(2,1)}), bf16[128,2,512]{2,1,0:T(2,128)(2,1)S(1)}, u32[]{:S(2)}, u32[]{:S(2)}) async-start(bf16[128,2,512]{2,1,0:T(2,128)(2,1)} %reshape.159), calls=%async_computation.3 | async-start | bytes 524288 | tf_op jit(solution)/shard_map/all_to_all | solution.py:104
  71.7 1.7 copy.56
  73.5 1.7 copy.32
  75.2 54.8 %while.10 = (s32[]{:T(128)}, bf16[4,64,256]{2,0,1:T(4,128)(2,1)}, s32[4]{0:T(128)}, s32[16,16]{1,0:T(8,128)}, bf16[64,48,256]{2,0,1:T(8,128)(2,1)}, /*index=5*/f...) while((s32[]{:T(128)}, bf16[4,64,256]{2,0,1:T(4,128)(2,1)}, ...), condition=%wide.region_1.2_spmd, body=%wide.region_0.1_spmd.sunk | while | flops 147084432 | bytes 3536671 | solution.py:63
  75.2 1.2 dynamic_slice.21
  80.3 1.3 constant_dynamic-slice_fusion.5
  81.7 2.0 gather_fusion.1
  83.7 3.6 %fusion.38 = bf16[1,64,256]{2,1,0:T(8,128)(2,1)S(1)} fusion(f32[16,256]{1,0:T(8,128)S(1)} %get-tuple-element.137, f32[16,256]{1,0:T(8,128)S(1)} %get-tuple-element.138, f32[256]{0:T(256)} %bitcast.153, f32[16,256]{1,0:T(8,128)S(1)} %get-tuple-element.142, f32[256]{0:T(256)} %bitcast.152, f32[16,256]{1,0:T(8,128)S(1)} %get-tuple-element.144, ...), kind=kOutput, calls=%fused_computation.8.clone.1 | convolution fusion | flops 147062784 | bytes 642064 | tf_op jit(solution)/shard_map/while/body/eval_jaxpr/npq,vnq->vp/dot_general | solution.py:61
  88.9 1.2 dynamic_slice.21
  94.0 1.3 constant_dynamic-slice_fusion.5
  95.4 2.0 gather_fusion.1
  97.4 3.6 %fusion.38 = bf16[1,64,256]{2,1,0:T(8,128)(2,1)S(1)} fusion(f32[16,256]{1,0:T(8,128)S(1)} %get-tuple-element.137, f32[16,256]{1,0:T(8,128)S(1)} %get-tuple-element.138, f32[256]{0:T(256)} %bitcast.153, f32[16,256]{1,0:T(8,128)S(1)} %get-tuple-element.142, f32[256]{0:T(256)} %bitcast.152, f32[16,256]{1,0:T(8,128)S(1)} %get-tuple-element.144, ...), kind=kOutput, calls=%fused_computation.8.clone.1 | convolution fusion | flops 147062784 | bytes 642064 | tf_op jit(solution)/shard_map/while/body/eval_jaxpr/npq,vnq->vp/dot_general | solution.py:61
  102.6 1.2 dynamic_slice.21
  107.7 1.3 constant_dynamic-slice_fusion.5
  109.1 2.0 gather_fusion.1
  111.1 3.6 %fusion.38 = bf16[1,64,256]{2,1,0:T(8,128)(2,1)S(1)} fusion(f32[16,256]{1,0:T(8,128)S(1)} %get-tuple-element.137, f32[16,256]{1,0:T(8,128)S(1)} %get-tuple-element.138, f32[256]{0:T(256)} %bitcast.153, f32[16,256]{1,0:T(8,128)S(1)} %get-tuple-element.142, f32[256]{0:T(256)} %bitcast.152, f32[16,256]{1,0:T(8,128)S(1)} %get-tuple-element.144, ...), kind=kOutput, calls=%fused_computation.8.clone.1 | convolution fusion | flops 147062784 | bytes 642064 | tf_op jit(solution)/shard_map/while/body/eval_jaxpr/npq,vnq->vp/dot_general | solution.py:61
  116.3 1.2 dynamic_slice.21
  121.4 1.3 constant_dynamic-slice_fusion.5
  122.8 2.0 gather_fusion.1
  124.8 3.6 %fusion.38 = bf16[1,64,256]{2,1,0:T(8,128)(2,1)S(1)} fusion(f32[16,256]{1,0:T(8,128)S(1)} %get-tuple-element.137, f32[16,256]{1,0:T(8,128)S(1)} %get-tuple-element.138, f32[256]{0:T(256)} %bitcast.153, f32[16,256]{1,0:T(8,128)S(1)} %get-tuple-element.142, f32[256]{0:T(256)} %bitcast.152, f32[16,256]{1,0:T(8,128)S(1)} %get-tuple-element.144, ...), kind=kOutput, calls=%fused_computation.8.clone.1 | convolution fusion | flops 147062784 | bytes 642064 | tf_op jit(solution)/shard_map/while/body/eval_jaxpr/npq,vnq->vp/dot_general | solution.py:61
  130.7 4.1 %all-to-all-start.1 = ((bf16[4,64,256]{2,0,1:T(4,128)(2,1)}), bf16[4,64,256]{2,0,1:T(4,128)(2,1)}, u32[]{:S(2)}, u32[]{:S(2)}) async-start(bf16[4,64,256]{2,0,1:T(4,128)(2,1)} %get-tuple-element.39), calls=%async_computation.1 | async-start | bytes 262144 | tf_op jit(solution)/shard_map/all_to_all | solution.py:112
  136.3 1.4 reshape.89
  137.7 3.2 %all-to-all-done.1 = bf16[4,64,256]{2,0,1:T(4,128)(2,1)} async-done(((bf16[4,64,256]{2,0,1:T(4,128)(2,1)}), bf16[4,64,256]{2,0,1:T(4,128)(2,1)}, u32[]{:S(2)}, u32[]{:S(2)}) %all-to-all-start.1) | async-done | bytes 131104 | tf_op jit(solution)/shard_map/all_to_all | solution.py:112
  140.9 16.6 %all-to-all-start.2 = ((bf16[128,2,1024]{2,1,0:T(2,128)(2,1)}), bf16[128,2,1024]{2,1,0:T(2,128)(2,1)}, u32[]{:S(2)}, u32[]{:S(2)}) async-start(bf16[128,2,1024]{2,1,0:T(2,128)(2,1)} %reshape.89), calls=%async_computation.2 | async-start | bytes 1048576 | tf_op jit(solution)/shard_map/all_to_all | solution.py:103
  157.7 2.2 %reshape.160 = bf16[128,1,1024]{2,1,0:T(2,128)(2,1)S(1)} reshape(bf16[128,2,512]{2,1,0:T(2,128)(2,1)} %copy-done.2) | data formatting | bytes 524288
  161.4 1.5 fusion.15
  163.0 0.9 copy.34
  163.9 26.2 %all-to-all-done.2 = bf16[128,2,1024]{2,1,0:T(2,128)(2,1)} async-done(((bf16[128,2,1024]{2,1,0:T(2,128)(2,1)}), bf16[128,2,1024]{2,1,0:T(2,128)(2,1)}, u32[]{:S(2)}, u32[]{:S(2)}) %all-to-all-start.2) | async-done | bytes 524320 | tf_op jit(solution)/shard_map/all_to_all | solution.py:103
  190.1 2.3 %reshape.90 = bf16[256,16,64]{2,1,0:T(8,128)(2,1)S(1)} reshape(bf16[128,2,1024]{2,1,0:T(2,128)(2,1)} %all-to-all-done.2) | data formatting | bytes 1048576 | tf_op jit(solution)/shard_map/reshape | solution.py:48
  192.4 1.8 gather_fusion.3
  194.2 4.0 %fusion.9 = bf16[16,16,256]{2,1,0:T(8,128)(2,1)S(1)} fusion(f32[16,16,256]{2,1,0:T(8,128)S(1)} %bitcast.140, bf16[16,64,256]{2,1,0:T(8,128)(2,1)} %param.19, f32[16,16,64]{2,1,0:T(8,128)} %bitcast.142, bf16[16,16,16,64]{3,2,1,0:T(8,128)(2,1)} %bitcast.132, bf16[16,16,64,64]{3,2,1,0:T(8,128)(2,1)} %param.21), kind=kOutput, calls=%fused_computation.31 | convolution fusion | flops 42106880 | bytes 3604480 | tf_op jit(solution)/shard_map/ikp,ivk->vip/dot_general | solution.py:123
  198.2 13.0 %all_to_all.29 = bf16[4,16,4096]{2,1,0:T(8,128)(2,1)S(1)} all-to-all(bf16[4,16,4096]{2,1,0:T(8,128)(2,1)S(1)} %broadcast_in_dim.59), channel_id=1, replica_groups=mesh['leaf'=128,'vec'=4] {'vec'}, dimensions={0} | all-to-all | bytes 1048576 | tf_op jit(solution)/shard_map/all_to_all | solution.py:32
  211.4 0.9 convolution_multiply_fusion
  (117 shorter events, 24.2 us)
Async XLA Ops:
  0.6 160.8 %copy-start = (bf16[8,16,64,64]{3,2,1,0:T(8,128)(2,1)S(1)}, bf16[8,16,64,64]{3,2,1,0:T(8,128)(2,1)}, u32[]{:S(2)}) copy-start(bf16[8,16,64,64]{3,2,1,0:T(8,128)(2,1)} %param.22) | copy-start | bytes 3145732
  0.6 25.9 %copy-start.5 = (bf16[16,4096]{1,0:T(8,128)(2,1)S(1)}, bf16[16,4096]{1,0:T(8,128)(2,1)}, u32[]{:S(2)}) copy-start(bf16[16,4096]{1,0:T(8,128)(2,1)} %param.15) | copy-start | bytes 393220
  0.7 25.9 %collective-permute-start.1 = (bf16[16,4096]{1,0:T(8,128)(2,1)}, bf16[16,4096]{1,0:T(8,128)(2,1)}, u32[]{:S(2)}, u32[]{:S(2)}) collective-permute-start(bf16[16,4096]{1,0:T(8,128)(2,1)} %param.15), channel_id=1, source_target_pairs={{4,0},{8,4},{12,8},{16,12},{20,16},{24,20},{28,24},{32,28},{36,32}... | collective-permute-start | bytes 393224 | tf_op jit(solution)/shard_map/ppermute | solution.py:19
  4.5 22.1 %collective-permute-start = (bf16[16,4096]{1,0:T(8,128)(2,1)}, bf16[16,4096]{1,0:T(8,128)(2,1)}, u32[]{:S(2)}, u32[]{:S(2)}) collective-permute-start(bf16[16,4096]{1,0:T(8,128)(2,1)} %param.15), channel_id=1, source_target_pairs={{0,4},{4,8},{8,12},{12,16},{16,20},{20,24},{24,28},{28,32},{32,36}... | collective-permute-start | bytes 393224 | tf_op jit(solution)/shard_map/ppermute | solution.py:16
  7.3 25.9 %collective-permute-start.3 = (f32[5,4096]{1,0:T(8,128)S(1)}, f32[5,4096]{1,0:T(8,128)S(1)}, u32[]{:S(2)}, u32[]{:S(2)}) collective-permute-start(f32[5,4096]{1,0:T(8,128)S(1)} %pad_maximum_fusion.2), channel_id=1, source_target_pairs={{4,0},{8,4},{12,8},{16,12},{20,16},{24,20},{28,24},{32,28},{36,32}... | collective-permute-start | bytes 245768 | tf_op jit(solution)/shard_map/ppermute | solution.py:19
  13.1 20.2 %collective-permute-start.2 = (f32[5,4096]{1,0:T(8,128)S(1)}, f32[5,4096]{1,0:T(8,128)}, u32[]{:S(2)}, u32[]{:S(2)}) collective-permute-start(f32[5,4096]{1,0:T(8,128)S(1)} %pad_maximum_fusion.2), channel_id=1, source_target_pairs={{0,4},{4,8},{8,12},{12,16},{16,20},{20,24},{24,28},{28,32},{32,36}... | collective-permute-start | bytes 245768 | tf_op jit(solution)/shard_map/ppermute | solution.py:16
  22.4 10.9 %copy-start.3 = (f32[3,4096]{1,0:T(4,128)S(1)}, f32[3,4096]{1,0:T(4,128)}, u32[]{:S(2)}) copy-start(f32[3,4096]{1,0:T(4,128)} %param.16) | copy-start | bytes 147460
  22.4 10.9 %copy-start.8 = (f32[4096]{0:T(1024)S(1)}, f32[4096]{0:T(1024)}, u32[]{:S(2)}) copy-start(f32[4096]{0:T(1024)} %param.18) | copy-start | bytes 49156
  28.8 23.3 %all-to-all-start = ((bf16[4,16,12288]{2,1,0:T(8,128)(2,1)}), bf16[4,16,12288]{2,1,0:T(8,128)(2,1)}, u32[]{:S(2)}, u32[]{:S(2)}) async-start(bf16[4,16,12288]{2,1,0:T(8,128)(2,1)} %broadcast_in_dim.52), calls=%async_computation | async-start | bytes 3145728 | tf_op jit(solution)/shard_map/all_to_all | solution.py:32
  52.1 77.9 %all-to-all-start.3 = ((bf16[128,2,512]{2,1,0:T(2,128)(2,1)}), bf16[128,2,512]{2,1,0:T(2,128)(2,1)S(1)}, u32[]{:S(2)}, u32[]{:S(2)}) async-start(bf16[128,2,512]{2,1,0:T(2,128)(2,1)} %reshape.159), calls=%async_computation.3 | async-start | bytes 524288 | tf_op jit(solution)/shard_map/all_to_all | solution.py:104
  80.1 1.5 copy-start.9
  83.7 3.7 %copy-start.6 = (bf16[4,64,256]{2,0,1:T(4,128)(2,1)S(1)}, bf16[4,64,256]{2,0,1:T(4,128)(2,1)}, u32[]{:S(2)}) copy-start(bf16[4,64,256]{2,0,1:T(4,128)(2,1)} %get-tuple-element.160) | copy-start | bytes 393220 | tf_op jit(solution)/shard_map/while
  88.3 0.7 copy-start.7
  93.8 1.5 copy-start.9
  97.4 3.7 %copy-start.6 = (bf16[4,64,256]{2,0,1:T(4,128)(2,1)S(1)}, bf16[4,64,256]{2,0,1:T(4,128)(2,1)}, u32[]{:S(2)}) copy-start(bf16[4,64,256]{2,0,1:T(4,128)(2,1)} %get-tuple-element.160) | copy-start | bytes 393220 | tf_op jit(solution)/shard_map/while
  102.0 0.7 copy-start.7
  107.5 1.5 copy-start.9
  111.1 3.7 %copy-start.6 = (bf16[4,64,256]{2,0,1:T(4,128)(2,1)S(1)}, bf16[4,64,256]{2,0,1:T(4,128)(2,1)}, u32[]{:S(2)}) copy-start(bf16[4,64,256]{2,0,1:T(4,128)(2,1)} %get-tuple-element.160) | copy-start | bytes 393220 | tf_op jit(solution)/shard_map/while
  115.7 0.7 copy-start.7
  121.2 1.5 copy-start.9
  124.8 3.7 %copy-start.6 = (bf16[4,64,256]{2,0,1:T(4,128)(2,1)S(1)}, bf16[4,64,256]{2,0,1:T(4,128)(2,1)}, u32[]{:S(2)}) copy-start(bf16[4,64,256]{2,0,1:T(4,128)(2,1)} %get-tuple-element.160) | copy-start | bytes 393220 | tf_op jit(solution)/shard_map/while
  129.4 0.7 copy-start.7
  130.0 27.4 %copy-start.11 = (s32[8,16]{1,0:T(8,128)S(1)}, s32[8,16]{1,0:T(8,128)}, u32[]{:S(2)}) copy-start(s32[8,16]{1,0:T(8,128)} %param.27) | copy-start | bytes 1540
  130.0 27.5 %copy-start.10 = (s32[16,16]{1,0:T(8,128)S(1)}, s32[16,16]{1,0:T(8,128)}, u32[]{:S(2)}) copy-start(s32[16,16]{1,0:T(8,128)} %param.26) | copy-start | bytes 3076
  130.0 0.7 copy-start.2
  130.7 30.7 %copy-start.1 = (bf16[8,2,64,64]{3,2,1,0:T(8,128)(2,1)S(1)}, bf16[8,2,64,64]{3,2,1,0:T(8,128)(2,1)}, u32[]{:S(2)}) copy-start(bf16[8,2,64,64]{3,2,1,0:T(8,128)(2,1)} %param.20) | copy-start | bytes 393220
  130.7 10.1 %all-to-all-start.1 = ((bf16[4,64,256]{2,0,1:T(4,128)(2,1)}), bf16[4,64,256]{2,0,1:T(4,128)(2,1)}, u32[]{:S(2)}, u32[]{:S(2)}) async-start(bf16[4,64,256]{2,0,1:T(4,128)(2,1)} %get-tuple-element.39), calls=%async_computation.1 | async-start | bytes 262144 | tf_op jit(solution)/shard_map/all_to_all | solution.py:112
  140.9 49.3 %all-to-all-start.2 = ((bf16[128,2,1024]{2,1,0:T(2,128)(2,1)}), bf16[128,2,1024]{2,1,0:T(2,128)(2,1)}, u32[]{:S(2)}, u32[]{:S(2)}) async-start(bf16[128,2,1024]{2,1,0:T(2,128)(2,1)} %reshape.89), calls=%async_computation.2 | async-start | bytes 1048576 | tf_op jit(solution)/shard_map/all_to_all | solution.py:103
  198.2 14.1 %copy-start.4 = (bf16[16,2,8,256]{3,2,0,1:T(8,128)(2,1)}, bf16[16,2,8,256]{3,2,0,1:T(8,128)(2,1)S(1)}, u32[]{:S(2)}) copy-start(bf16[16,2,8,256]{3,2,0,1:T(8,128)(2,1)S(1)} %copy.55) | copy-start | bytes 393220
where the time goes:
time: 214 us; the launch traced here: 212 us
  starting transfers between devices  58.1 us (27%)
  local copies, waits for them, and re-layouts  48.9 us (23%)
  waiting for transfers between devices  47.2 us (22%)
  matrix products  23.4 us (11%)
  other arithmetic  13.4 us (6%)
  blocking collectives  13 us (6%)
  loops' own time  7.29 us (3%)
    all_to_all x1, waiting for transfers between devices, per_device(): lax.all_to_all(send_leafs, 'leaf', split_axis=0, concat_axis=0, tiled=True)  26.2 us
    all_to_all x1, starting transfers between devices, per_device(): lax.all_to_all(send_parents, 'leaf', split_axis=0, concat_axis=0, tiled=T...  19.6 us
    all_to_all x1, waiting for transfers between devices, copy_for_each(): return lax.all_to_all(copies, axis, split_axis=0, concat_axis=0, tiled=True)  17.8 us
    all_to_all x1, starting transfers between devices, per_device(): lax.all_to_all(send_leafs, 'leaf', split_axis=0, concat_axis=0, tiled=True)  16.6 us
    dot_general x4, matrix products, one_leaf(): jnp.einsum('npq,vnq->vp', blocks, src_vec, preferred_element_type=jnp.flo...  14.5 us
    all_to_all x1, blocking collectives, copy_for_each(): return lax.all_to_all(copies, axis, split_axis=0, concat_axis=0, tiled=True)  13 us
    ppermute x2, starting transfers between devices, extended(): lax.ppermute(lax.slice_in_dim(block, 0, width, axis=dim), axis, backward)  9.54 us
    gather x4, local copies, waits for them, and re-layouts, one_leaf(): src_vec = jnp.take(vec_leaves, chosen, axis=1)  7.95 us
  transfers between devices with their start and end apart: 8, of which 3 were waited for; matrix products, arithmetic and copies ran while one was open for 34% of the time, Pallas kernels for 0%

commit v1 on v0

--- a/solution.py
+++ b/solution.py
@@ -6,6 +6,29 @@
 LEAF = 256
 HW = 16
 four_pi = 4.0 * 3.141592653589793
+
+
+def in_blocks(shard, dim, size):
+    before, after = (shard.shape[:dim], shard.shape[dim + 1 :])
+    return jnp.moveaxis(shard.reshape(*before, size, -1, *after), dim, 0)
+
+
+def laid_out_2(tiles, dim):
+    tiles = jnp.moveaxis(tiles, 0, dim)
+    shape = tiles.shape
+    return tiles.reshape(*shape[:dim], shape[dim] * shape[dim + 1], *shape[dim + 2 :])
+
+
+def rotated_exchange(value, axis, split_dim, concat_dim):
+    size, mine = (lax.axis_size(axis), lax.axis_index(axis))
+    blocks = in_blocks(value, split_dim, size)
+    filled = blocks
+    for step in range(1, size):
+        target, source = ((mine + step) % size, (mine - step) % size)
+        sent = lax.dynamic_index_in_dim(blocks, target, 0)
+        partner_block = lax.ppermute(sent, axis, [(i, (i + step) % size) for i in range(size)])
+        filled = lax.dynamic_update_slice_in_dim(filled, partner_block, source, axis=0)
+    return laid_out_2(filled, concat_dim)
 
 
 def extended(block, sides, width):
@@ -109,9 +132,9 @@
     first_leaf = lax.axis_index("vec") * quarter
     leaf_ids = first_leaf + jnp.arange(quarter, dtype=jnp.int32)
     near_quarter = near_leaves(leaf_ids, window, geo_leaves, all_leaves, targets)
-    near_part = lax.all_to_all(
-        near_quarter.astype(jnp.bfloat16), "vec", split_axis=1, concat_axis=0, tiled=True
-    ).astype(near_quarter.dtype)
+    near_part = rotated_exchange(near_quarter.astype(jnp.bfloat16), "vec", 1, 0).astype(
+        near_quarter.dtype
+    )
     field_fine = apply_coupling(coupling_fine, got_leafs, far_fine, vec_dev, basis_rank)
     field_coarse = apply_coupling(
         coupling_coarse, got_parents, far_coarse, vec_dev, basis_rank

time: 214 us -> 199 us (0.930)
  the two profiles are of different devices: /device:TPU:32 before, /device:TPU:2 now
where the time goes in v1:
time: 199 us; the launch traced here: 197 us
  starting transfers between devices  56.1 us (28%)
  local copies, waits for them, and re-layouts  46.5 us (23%)
  waiting for transfers between devices  34.3 us (17%)
  matrix products  26.4 us (13%)
  other arithmetic  13.3 us (7%)
  blocking collectives  11.3 us (6%)
  loops' own time  7.96 us (4%)
    all_to_all x1, starting transfers between devices, per_device(): lax.all_to_all(send_parents, 'leaf', split_axis=0, concat_axis=0, tiled=T...  21.3 us
    dot_general x4, matrix products, one_leaf(): jnp.einsum('npq,vnq->vp', blocks, src_vec, preferred_element_type=jnp.flo...  17.2 us
    all_to_all x1, waiting for transfers between devices, copy_for_each(): return lax.all_to_all(copies, axis, split_axis=0, concat_axis=0, tiled=True)  16.6 us
    all_to_all x1, waiting for transfers between devices, per_device(): lax.all_to_all(send_parents, 'leaf', split_axis=0, concat_axis=0, tiled=T...  14.5 us
    all_to_all x1, blocking collectives, copy_for_each(): return lax.all_to_all(copies, axis, split_axis=0, concat_axis=0, tiled=True)  11.3 us
    ppermute x2, starting transfers between devices, extended(): lax.ppermute(lax.slice_in_dim(block, 0, width, axis=dim), axis, backward)  9.48 us
    ppermute x3, starting transfers between devices, rotated_exchange(): lax.ppermute(sent, axis, [(i, (i + step) % size) for i in range(size)])  9.04 us
    gather x4, local copies, waits for them, and re-layouts, one_leaf(): src_vec = jnp.take(vec_leaves, chosen, axis=1)  8.44 us
  transfers between devices with their start and end apart: 10, of which 4 were waited for; matrix products, arithmetic and copies ran while one was open for 39% of the time, Pallas kernels for 0%

profile of v1, /device:TPU:2, one launch (start us, length us, event | category | flops | bytes accessed | tf_op | source)
XLA Modules:
  0.0 196.9 jit_solution(17494450268549482725)
XLA Ops:
  0.7 2.1 %collective-permute-start.1 = (bf16[16,4096]{1,0:T(8,128)(2,1)}, bf16[16,4096]{1,0:T(8,128)(2,1)}, u32[]{:S(2)}, u32[]{:S(2)}) collective-permute-start(bf16[16,4096]{1,0:T(8,128)(2,1)} %param.15), channel_id=1, source_target_pairs={{4,0},{8,4},{12,8},{16,12},{20,16},{24,20},{28,24},{32,28},{36,32}... | collective-permute-start | bytes 393224 | tf_op jit(solution)/shard_map/ppermute | solution.py:42
  2.8 2.4 %collective-permute-start = (bf16[16,4096]{1,0:T(8,128)(2,1)}, bf16[16,4096]{1,0:T(8,128)(2,1)}, u32[]{:S(2)}, u32[]{:S(2)}) collective-permute-start(bf16[16,4096]{1,0:T(8,128)(2,1)} %param.15), channel_id=1, source_target_pairs={{0,4},{4,8},{8,12},{12,16},{16,20},{20,24},{24,28},{28,32},{32,36}... | collective-permute-start | bytes 393224 | tf_op jit(solution)/shard_map/ppermute | solution.py:39
  5.2 1.6 pad_maximum_fusion.2
  6.8 7.4 %collective-permute-start.3 = (f32[5,4096]{1,0:T(8,128)}, f32[5,4096]{1,0:T(8,128)}, u32[]{:S(2)}, u32[]{:S(2)}) collective-permute-start(f32[5,4096]{1,0:T(8,128)} %pad_maximum_fusion.2), channel_id=1, source_target_pairs={{4,0},{8,4},{12,8},{16,12},{20,16},{24,20},{28,24},{32,28},{36,32}... | collective-permute-start | bytes 245768 | tf_op jit(solution)/shard_map/ppermute | solution.py:42
  14.2 1.9 collective-permute-start.2
  16.8 1.3 convolution_convert_fusion
  18.1 1.2 fusion.13
  22.0 0.9 reshape.164
  22.9 21.3 %all-to-all-start.2 = ((bf16[128,2,512]{2,1,0:T(2,128)(2,1)}), bf16[128,2,512]{2,1,0:T(2,128)(2,1)S(1)}, u32[]{:S(2)}, u32[]{:S(2)}) async-start(bf16[128,2,512]{2,1,0:T(2,128)(2,1)} %reshape.164), calls=%async_computation.2 | async-start | bytes 524288 | tf_op jit(solution)/shard_map/all_to_all | solution.py:127
  47.9 1.4 reshape.95
  50.0 1.1 pad_maximum_fusion
  51.0 14.5 %all-to-all-done.2 = bf16[128,2,512]{2,1,0:T(2,128)(2,1)S(1)} async-done(((bf16[128,2,512]{2,1,0:T(2,128)(2,1)}), bf16[128,2,512]{2,1,0:T(2,128)(2,1)S(1)}, u32[]{:S(2)}, u32[]{:S(2)}) %all-to-all-start.2) | async-done | bytes 262176 | tf_op jit(solution)/shard_map/all_to_all | solution.py:127
  65.5 1.2 broadcast_in_dim.52
  66.7 4.5 %all-to-all-start = ((bf16[4,16,12288]{2,1,0:T(8,128)(2,1)}), bf16[4,16,12288]{2,1,0:T(8,128)(2,1)}, u32[]{:S(2)}, u32[]{:S(2)}) async-start(bf16[4,16,12288]{2,1,0:T(8,128)(2,1)} %broadcast_in_dim.52), calls=%async_computation | async-start | bytes 3145728 | tf_op jit(solution)/shard_map/all_to_all | solution.py:55
  71.2 1.0 pad_maximum_fusion.1
  72.3 2.2 %reshape.165 = bf16[128,1,1024]{2,1,0:T(2,128)(2,1)S(1)} reshape(bf16[128,2,512]{2,1,0:T(2,128)(2,1)} %copy-done.1) | data formatting | bytes 524288
  76.2 16.6 %all-to-all-done = bf16[4,16,12288]{2,1,0:T(8,128)(2,1)} async-done(((bf16[4,16,12288]{2,1,0:T(8,128)(2,1)}), bf16[4,16,12288]{2,1,0:T(8,128)(2,1)}, u32[]{:S(2)}, u32[]{:S(2)}) %all-to-all-start) | async-done | bytes 1572896 | tf_op jit(solution)/shard_map/all_to_all | solution.py:55
  92.7 7.4 %all-to-all-start.1 = ((bf16[128,2,1024]{2,1,0:T(2,128)(2,1)}), bf16[128,2,1024]{2,1,0:T(2,128)(2,1)}, u32[]{:S(2)}, u32[]{:S(2)}) async-start(bf16[128,2,1024]{2,1,0:T(2,128)(2,1)} %reshape.95), calls=%async_computation.1 | async-start | bytes 1048576 | tf_op jit(solution)/shard_map/all_to_all | solution.py:126
  100.2 1.7 copy.53
  101.9 1.8 copy.32
  103.7 57.0 %while.10 = (s32[]{:T(128)}, bf16[4,64,256]{2,1,0:T(8,128)(2,1)}, s32[4]{0:T(128)}, s32[16,16]{1,0:T(8,128)}, bf16[64,48,256]{2,0,1:T(8,128)(2,1)}, /*index=5*/f...) while((s32[]{:T(128)}, bf16[4,64,256]{2,1,0:T(8,128)(2,1)}, ...), condition=%wide.region_1.2_spmd, body=%wide.region_0.1_spmd.sunk | while | flops 147084432 | bytes 2406643 | solution.py:86
  103.7 1.2 dynamic_slice.34
  109.5 1.3 constant_dynamic-slice_fusion.5
  111.5 2.1 %gather_fusion.1 = bf16[16,64,256]{2,1,0:T(8,128)(2,1)S(1)} fusion(bf16[64,48,256]{2,0,1:T(8,128)(2,1)} %get-tuple-element.178, s32[1024]{0:T(1024)} %copy-done.5), kind=kCustom, calls=%fused_computation.clone.1 | custom fusion | bytes 1048640 | tf_op jit(solution)/shard_map/while/body/eval_jaxpr/jit(_take)/gather | solution.py:81
  113.6 4.3 %fusion.40 = bf16[4,64,256]{2,1,0:T(8,128)(2,1)} fusion(bf16[4,64,256]{2,1,0:T(8,128)(2,1)} %get-tuple-element.163, s32[]{:T(128)S(6)} %copy.82, f32[16,256]{1,0:T(8,128)} %get-tuple-element.140, f32[16,256]{1,0:T(8,128)} %get-tuple-element.141, f32[256]{0:T(256)} %bitcast.167, f32[16,256]{1,0:T(8,128)} %get-tuple-element.145, f32[256]{0:T(256)} %bitcast.166, ...), kind=kOutput, calls=%fused_computation.9.clone.1 | convolution fusion | flops 147062784 | bytes 675332 | tf_op jit(solution)/shard_map/while/body/eval_jaxpr/npq,vnq->vp/dot_general | solution.py:84
  117.9 1.2 dynamic_slice.34
  123.8 1.3 constant_dynamic-slice_fusion.5
  125.7 2.1 %gather_fusion.1 = bf16[16,64,256]{2,1,0:T(8,128)(2,1)S(1)} fusion(bf16[64,48,256]{2,0,1:T(8,128)(2,1)} %get-tuple-element.178, s32[1024]{0:T(1024)} %copy-done.5), kind=kCustom, calls=%fused_computation.clone.1 | custom fusion | bytes 1048640 | tf_op jit(solution)/shard_map/while/body/eval_jaxpr/jit(_take)/gather | solution.py:81
  127.9 4.3 %fusion.40 = bf16[4,64,256]{2,1,0:T(8,128)(2,1)} fusion(bf16[4,64,256]{2,1,0:T(8,128)(2,1)} %get-tuple-element.163, s32[]{:T(128)S(6)} %copy.82, f32[16,256]{1,0:T(8,128)} %get-tuple-element.140, f32[16,256]{1,0:T(8,128)} %get-tuple-element.141, f32[256]{0:T(256)} %bitcast.167, f32[16,256]{1,0:T(8,128)} %get-tuple-element.145, f32[256]{0:T(256)} %bitcast.166, ...), kind=kOutput, calls=%fused_computation.9.clone.1 | convolution fusion | flops 147062784 | bytes 675332 | tf_op jit(solution)/shard_map/while/body/eval_jaxpr/npq,vnq->vp/dot_general | solution.py:84
  132.2 1.2 dynamic_slice.34
  138.0 1.3 constant_dynamic-slice_fusion.5
  140.0 2.1 %gather_fusion.1 = bf16[16,64,256]{2,1,0:T(8,128)(2,1)S(1)} fusion(bf16[64,48,256]{2,0,1:T(8,128)(2,1)} %get-tuple-element.178, s32[1024]{0:T(1024)} %copy-done.5), kind=kCustom, calls=%fused_computation.clone.1 | custom fusion | bytes 1048640 | tf_op jit(solution)/shard_map/while/body/eval_jaxpr/jit(_take)/gather | solution.py:81
  142.1 4.3 %fusion.40 = bf16[4,64,256]{2,1,0:T(8,128)(2,1)} fusion(bf16[4,64,256]{2,1,0:T(8,128)(2,1)} %get-tuple-element.163, s32[]{:T(128)S(6)} %copy.82, f32[16,256]{1,0:T(8,128)} %get-tuple-element.140, f32[16,256]{1,0:T(8,128)} %get-tuple-element.141, f32[256]{0:T(256)} %bitcast.167, f32[16,256]{1,0:T(8,128)} %get-tuple-element.145, f32[256]{0:T(256)} %bitcast.166, ...), kind=kOutput, calls=%fused_computation.9.clone.1 | convolution fusion | flops 147062784 | bytes 675332 | tf_op jit(solution)/shard_map/while/body/eval_jaxpr/npq,vnq->vp/dot_general | solution.py:84
  146.4 1.2 dynamic_slice.34
  152.3 1.3 constant_dynamic-slice_fusion.5
  154.2 2.1 %gather_fusion.1 = bf16[16,64,256]{2,1,0:T(8,128)(2,1)S(1)} fusion(bf16[64,48,256]{2,0,1:T(8,128)(2,1)} %get-tuple-element.178, s32[1024]{0:T(1024)} %copy-done.5), kind=kCustom, calls=%fused_computation.clone.1 | custom fusion | bytes 1048640 | tf_op jit(solution)/shard_map/while/body/eval_jaxpr/jit(_take)/gather | solution.py:81
  156.4 4.3 %fusion.40 = bf16[4,64,256]{2,1,0:T(8,128)(2,1)} fusion(bf16[4,64,256]{2,1,0:T(8,128)(2,1)} %get-tuple-element.163, s32[]{:T(128)S(6)} %copy.82, f32[16,256]{1,0:T(8,128)} %get-tuple-element.140, f32[16,256]{1,0:T(8,128)} %get-tuple-element.141, f32[256]{0:T(256)} %bitcast.167, f32[16,256]{1,0:T(8,128)} %get-tuple-element.145, f32[256]{0:T(256)} %bitcast.166, ...), kind=kOutput, calls=%fused_computation.9.clone.1 | convolution fusion | flops 147062784 | bytes 675332 | tf_op jit(solution)/shard_map/while/body/eval_jaxpr/npq,vnq->vp/dot_general | solution.py:84
  161.5 2.5 %collective-permute-start.4 = (bf16[1,4,16,256]{3,2,1,0:T(8,128)(2,1)S(1)}, bf16[1,4,16,256]{3,2,1,0:T(8,128)(2,1)S(1)}, u32[]{:S(2)}, u32[]{:S(2)}) collective-permute-start(bf16[1,4,16,256]{3,2,1,0:T(8,128)(2,1)S(1)} %get-tuple-element.82), channel_id=1, source_target_pairs={{0,1},{1,2},{2,3},{3,0},{4,5},{5,6},{6,7},{7,4},{8,9},{9,10},{10,1... | collective-permute-start | bytes 98312 | tf_op jit(solution)/shard_map/ppermute | solution.py:29
  164.0 1.8 fusion.16
  165.8 0.9 copy.70
  166.8 4.0 %collective-permute-start.5 = (bf16[1,4,16,256]{3,2,1,0:T(8,128)(2,1)S(1)}, bf16[1,4,16,256]{3,2,1,0:T(8,128)(2,1)S(1)}, u32[]{:S(2)}, u32[]{:S(2)}) collective-permute-start(bf16[1,4,16,256]{3,2,1,0:T(8,128)(2,1)S(1)} %get-tuple-element.81), channel_id=1, source_target_pairs={{0,2},{1,3},{2,0},{3,1},{4,6},{5,7},{6,4},{7,5},{8,10},{9,11},{10,... | collective-permute-start | bytes 98312 | tf_op jit(solution)/shard_map/ppermute | solution.py:29
  170.7 2.5 %collective-permute-start.6 = (bf16[1,4,16,256]{3,2,1,0:T(8,128)(2,1)S(1)}, bf16[1,4,16,256]{3,2,1,0:T(8,128)(2,1)S(1)}, u32[]{:S(2)}, u32[]{:S(2)}) collective-permute-start(bf16[1,4,16,256]{3,2,1,0:T(8,128)(2,1)S(1)} %get-tuple-element.80), channel_id=1, source_target_pairs={{0,3},{1,0},{2,1},{3,2},{4,7},{5,4},{6,5},{7,6},{8,11},{9,8},{10,9... | collective-permute-start | bytes 98312 | tf_op jit(solution)/shard_map/ppermute | solution.py:29
  174.1 2.5 %collective-permute-done.6 = bf16[1,4,16,256]{3,2,1,0:T(8,128)(2,1)S(1)} collective-permute-done((bf16[1,4,16,256]{3,2,1,0:T(8,128)(2,1)S(1)}, bf16[1,4,16,256]{3,2,1,0:T(8,128)(2,1)S(1)}, u32[]{:S(2)}, u32[]{:S(2)}) %collective-permute-start.6) | collective-permute-done | bytes 32800 | tf_op jit(solution)/shard_map/ppermute | solution.py:29
  176.5 2.3 %reshape.96 = bf16[256,16,64]{2,1,0:T(8,128)(2,1)S(1)} reshape(bf16[128,2,1024]{2,1,0:T(2,128)(2,1)} %all-to-all-done.1) | data formatting | bytes 1048576 | tf_op jit(solution)/shard_map/reshape | solution.py:71
  178.8 1.8 gather_fusion.3
  180.6 3.9 %fusion.18 = bf16[16,16,256]{2,1,0:T(8,128)(2,1)S(1)} fusion(bf16[4,4,16,256]{3,2,1,0:T(8,128)(2,1)S(1)} %constant_dynamic-update-slice_fusion, bf16[16,64,256]{2,1,0:T(8,128)(2,1)} %param.19, f32[16,16,64]{2,1,0:T(8,128)S(1)} %bitcast.153, bf16[16,16,16,64]{3,2,1,0:T(8,128)(2,1)} %bitcast.144, bf16[16,16,64,64]{3,2,1,0:T(8,128)(2,1)} %param.21), kind=kOutput, calls=%fused_computation.47 | convolution fusion | flops 42172416 | bytes 3473408 | tf_op jit(solution)/shard_map/ikp,ivk->vip/dot_general | solution.py:146
  184.6 11.3 %all_to_all.20 = bf16[4,16,4096]{2,1,0:T(8,128)(2,1)S(1)} all-to-all(bf16[4,16,4096]{2,1,0:T(8,128)(2,1)S(1)} %broadcast_in_dim.59), channel_id=1, replica_groups=mesh['leaf'=128,'vec'=4] {'vec'}, dimensions={0} | all-to-all | bytes 1048576 | tf_op jit(solution)/shard_map/all_to_all | solution.py:55
  196.0 0.9 convolution_multiply_fusion
  (115 shorter events, 24.3 us)
Async XLA Ops:
  0.6 163.4 %copy-start = (bf16[8,16,64,64]{3,2,1,0:T(8,128)(2,1)S(1)}, bf16[8,16,64,64]{3,2,1,0:T(8,128)(2,1)}, u32[]{:S(2)}) copy-start(bf16[8,16,64,64]{3,2,1,0:T(8,128)(2,1)} %param.22) | copy-start | bytes 3145732
  0.6 45.7 %copy-start.2 = (f32[3,4096]{1,0:T(4,128)S(1)}, f32[3,4096]{1,0:T(4,128)}, u32[]{:S(2)}) copy-start(f32[3,4096]{1,0:T(4,128)} %param.16) | copy-start | bytes 147460
  0.7 43.6 %copy-start.12 = (s32[8,16]{1,0:T(8,128)S(1)}, s32[8,16]{1,0:T(8,128)}, u32[]{:S(2)}) copy-start(s32[8,16]{1,0:T(8,128)} %param.27) | copy-start | bytes 1540
  0.7 44.3 %copy-start.13 = (s32[128,2]{0,1:T(2,128)S(1)}, s32[128,2]{0,1:T(2,128)}, u32[]{:S(2)}) copy-start(s32[128,2]{0,1:T(2,128)} %param.24) | copy-start | bytes 3076
  0.7 44.5 %copy-start.10 = (s32[16,16]{1,0:T(8,128)S(1)}, s32[16,16]{1,0:T(8,128)}, u32[]{:S(2)}) copy-start(s32[16,16]{1,0:T(8,128)} %param.26) | copy-start | bytes 3076
  0.7 44.6 %copy-start.11 = (s32[16,16]{1,0:T(8,128)S(1)}, s32[16,16]{1,0:T(8,128)}, u32[]{:S(2)}) copy-start(s32[16,16]{1,0:T(8,128)} %param.23) | copy-start | bytes 3076
  0.7 49.3 %collective-permute-start.1 = (bf16[16,4096]{1,0:T(8,128)(2,1)}, bf16[16,4096]{1,0:T(8,128)(2,1)}, u32[]{:S(2)}, u32[]{:S(2)}) collective-permute-start(bf16[16,4096]{1,0:T(8,128)(2,1)} %param.15), channel_id=1, source_target_pairs={{4,0},{8,4},{12,8},{16,12},{20,16},{24,20},{28,24},{32,28},{36,32}... | collective-permute-start | bytes 393224 | tf_op jit(solution)/shard_map/ppermute | solution.py:42
  2.8 47.2 %collective-permute-start = (bf16[16,4096]{1,0:T(8,128)(2,1)}, bf16[16,4096]{1,0:T(8,128)(2,1)}, u32[]{:S(2)}, u32[]{:S(2)}) collective-permute-start(bf16[16,4096]{1,0:T(8,128)(2,1)} %param.15), channel_id=1, source_target_pairs={{0,4},{4,8},{8,12},{12,16},{16,20},{20,24},{24,28},{28,32},{32,36}... | collective-permute-start | bytes 393224 | tf_op jit(solution)/shard_map/ppermute | solution.py:39
  6.8 64.4 %collective-permute-start.3 = (f32[5,4096]{1,0:T(8,128)}, f32[5,4096]{1,0:T(8,128)}, u32[]{:S(2)}, u32[]{:S(2)}) collective-permute-start(f32[5,4096]{1,0:T(8,128)} %pad_maximum_fusion.2), channel_id=1, source_target_pairs={{4,0},{8,4},{12,8},{16,12},{20,16},{24,20},{28,24},{32,28},{36,32}... | collective-permute-start | bytes 245768 | tf_op jit(solution)/shard_map/ppermute | solution.py:42
  14.2 57.0 %collective-permute-start.2 = (f32[5,4096]{1,0:T(8,128)}, f32[5,4096]{1,0:T(8,128)}, u32[]{:S(2)}, u32[]{:S(2)}) collective-permute-start(f32[5,4096]{1,0:T(8,128)} %pad_maximum_fusion.2), channel_id=1, source_target_pairs={{0,4},{4,8},{8,12},{12,16},{16,20},{20,24},{24,28},{28,32},{32,36}... | collective-permute-start | bytes 245768 | tf_op jit(solution)/shard_map/ppermute | solution.py:39
  22.9 42.6 %all-to-all-start.2 = ((bf16[128,2,512]{2,1,0:T(2,128)(2,1)}), bf16[128,2,512]{2,1,0:T(2,128)(2,1)S(1)}, u32[]{:S(2)}, u32[]{:S(2)}) async-start(bf16[128,2,512]{2,1,0:T(2,128)(2,1)} %reshape.164), calls=%async_computation.2 | async-start | bytes 524288 | tf_op jit(solution)/shard_map/all_to_all | solution.py:127
  47.9 23.4 %copy-start.6 = (f32[4096]{0:T(1024)S(1)}, f32[4096]{0:T(1024)}, u32[]{:S(2)}) copy-start(f32[4096]{0:T(1024)} %param.18) | copy-start | bytes 49156
  49.3 22.0 %copy-start.3 = (f32[3,4096]{1,0:T(4,128)S(1)}, f32[3,4096]{1,0:T(4,128)}, u32[]{:S(2)}) copy-start(f32[3,4096]{1,0:T(4,128)} %param.16) | copy-start | bytes 147460
  49.3 22.0 %copy-start.7 = (f32[4096]{0:T(1024)S(1)}, f32[4096]{0:T(1024)}, u32[]{:S(2)}) copy-start(f32[4096]{0:T(1024)} %param.17) | copy-start | bytes 49156
  65.5 5.7 %copy-start.1 = (bf16[128,2,512]{2,1,0:T(2,128)(2,1)}, bf16[128,2,512]{2,1,0:T(2,128)(2,1)S(1)}, u32[]{:S(2)}) copy-start(bf16[128,2,512]{2,1,0:T(2,128)(2,1)S(1)} %all-to-all-done.2) | copy-start | bytes 786436
  66.7 26.0 %all-to-all-start = ((bf16[4,16,12288]{2,1,0:T(8,128)(2,1)}), bf16[4,16,12288]{2,1,0:T(8,128)(2,1)}, u32[]{:S(2)}, u32[]{:S(2)}) async-start(bf16[4,16,12288]{2,1,0:T(8,128)(2,1)} %broadcast_in_dim.52), calls=%async_computation | async-start | bytes 3145728 | tf_op jit(solution)/shard_map/all_to_all | solution.py:55
  92.7 83.8 %all-to-all-start.1 = ((bf16[128,2,1024]{2,1,0:T(2,128)(2,1)}), bf16[128,2,1024]{2,1,0:T(2,128)(2,1)}, u32[]{:S(2)}, u32[]{:S(2)}) async-start(bf16[128,2,1024]{2,1,0:T(2,128)(2,1)} %reshape.95), calls=%async_computation.1 | async-start | bytes 1048576 | tf_op jit(solution)/shard_map/all_to_all | solution.py:126
  107.5 4.0 %copy-start.5 = (s32[1024]{0:T(1024)}, s32[1024]{0:T(1024)S(1)}, u32[]{:S(2)}) copy-start(s32[1024]{0:T(1024)S(1)} %pad_clamp_fusion.6) | copy-start | bytes 12292 | tf_op jit(solution)/shard_map/while
  108.8 2.7 %copy-start.9 = (pred[16]{0:T(512)(128)(4,1)}, pred[16]{0:T(512)(128)(4,1)S(1)}, u32[]{:S(2)}) copy-start(pred[16]{0:T(512)(128)(4,1)S(1)} %compare_and_fusion.2) | copy-start | bytes 52 | tf_op jit(solution)/shard_map/while
  121.7 4.0 %copy-start.5 = (s32[1024]{0:T(1024)}, s32[1024]{0:T(1024)S(1)}, u32[]{:S(2)}) copy-start(s32[1024]{0:T(1024)S(1)} %pad_clamp_fusion.6) | copy-start | bytes 12292 | tf_op jit(solution)/shard_map/while
  123.0 2.7 %copy-start.9 = (pred[16]{0:T(512)(128)(4,1)}, pred[16]{0:T(512)(128)(4,1)S(1)}, u32[]{:S(2)}) copy-start(pred[16]{0:T(512)(128)(4,1)S(1)} %compare_and_fusion.2) | copy-start | bytes 52 | tf_op jit(solution)/shard_map/while
  136.0 4.0 %copy-start.5 = (s32[1024]{0:T(1024)}, s32[1024]{0:T(1024)S(1)}, u32[]{:S(2)}) copy-start(s32[1024]{0:T(1024)S(1)} %pad_clamp_fusion.6) | copy-start | bytes 12292 | tf_op jit(solution)/shard_map/while
  137.3 2.7 %copy-start.9 = (pred[16]{0:T(512)(128)(4,1)}, pred[16]{0:T(512)(128)(4,1)S(1)}, u32[]{:S(2)}) copy-start(pred[16]{0:T(512)(128)(4,1)S(1)} %compare_and_fusion.2) | copy-start | bytes 52 | tf_op jit(solution)/shard_map/while
  150.2 4.0 %copy-start.5 = (s32[1024]{0:T(1024)}, s32[1024]{0:T(1024)S(1)}, u32[]{:S(2)}) copy-start(s32[1024]{0:T(1024)S(1)} %pad_clamp_fusion.6) | copy-start | bytes 12292 | tf_op jit(solution)/shard_map/while
  151.5 2.7 %copy-start.9 = (pred[16]{0:T(512)(128)(4,1)}, pred[16]{0:T(512)(128)(4,1)S(1)}, u32[]{:S(2)}) copy-start(pred[16]{0:T(512)(128)(4,1)S(1)} %compare_and_fusion.2) | copy-start | bytes 52 | tf_op jit(solution)/shard_map/while
  160.7 18.1 %copy-start.8 = (s32[1024]{0:T(1024)S(1)}, s32[1024]{0:T(1024)}, u32[]{:S(2)}) copy-start(s32[1024]{0:T(1024)} %pad_clamp_fusion.3) | copy-start | bytes 12292
  161.5 11.8 %collective-permute-start.4 = (bf16[1,4,16,256]{3,2,1,0:T(8,128)(2,1)S(1)}, bf16[1,4,16,256]{3,2,1,0:T(8,128)(2,1)S(1)}, u32[]{:S(2)}, u32[]{:S(2)}) collective-permute-start(bf16[1,4,16,256]{3,2,1,0:T(8,128)(2,1)S(1)} %get-tuple-element.82), channel_id=1, source_target_pairs={{0,1},{1,2},{2,3},{3,0},{4,5},{5,6},{6,7},{7,4},{8,9},{9,10},{10,1... | collective-permute-start | bytes 98312 | tf_op jit(solution)/shard_map/ppermute | solution.py:29
  166.8 7.3 %collective-permute-start.5 = (bf16[1,4,16,256]{3,2,1,0:T(8,128)(2,1)S(1)}, bf16[1,4,16,256]{3,2,1,0:T(8,128)(2,1)S(1)}, u32[]{:S(2)}, u32[]{:S(2)}) collective-permute-start(bf16[1,4,16,256]{3,2,1,0:T(8,128)(2,1)S(1)} %get-tuple-element.81), channel_id=1, source_target_pairs={{0,2},{1,3},{2,0},{3,1},{4,6},{5,7},{6,4},{7,5},{8,10},{9,11},{10,... | collective-permute-start | bytes 98312 | tf_op jit(solution)/shard_map/ppermute | solution.py:29
  170.7 5.8 %collective-permute-start.6 = (bf16[1,4,16,256]{3,2,1,0:T(8,128)(2,1)S(1)}, bf16[1,4,16,256]{3,2,1,0:T(8,128)(2,1)S(1)}, u32[]{:S(2)}, u32[]{:S(2)}) collective-permute-start(bf16[1,4,16,256]{3,2,1,0:T(8,128)(2,1)S(1)} %get-tuple-element.80), channel_id=1, source_target_pairs={{0,3},{1,0},{2,1},{3,2},{4,7},{5,4},{6,5},{7,6},{8,11},{9,8},{10,9... | collective-permute-start | bytes 98312 | tf_op jit(solution)/shard_map/ppermute | solution.py:29
  184.5 12.4 %copy-start.4 = (bf16[16,2,8,256]{3,2,0,1:T(8,128)(2,1)}, bf16[16,2,8,256]{3,2,0,1:T(8,128)(2,1)S(1)}, u32[]{:S(2)}) copy-start(bf16[16,2,8,256]{3,2,0,1:T(8,128)(2,1)S(1)} %copy.52) | copy-start | bytes 393220
